TPU v7x, 32 devices: a whole 2x2x4 slice. The times are simulated.
32 devices in a mesh: row: 8 (over z, core), col: 4 (over y, x).
Axes of the slice: x: 2, y: 2, z: 4, core: 2. Of those that a mesh axis runs over, the one named last changes fastest.
Arguments:
- amplitudes: float32 [16, 16, 160, 160], P('row', 'col'), may hold values from -8 to 8, as said below
- vvvv: float32 [160, 160, 160, 160], P('row', None, 'col'), may hold values from -0.0390625 to 0.0390625
- hole_ints: float32 [16, 16, 16, 16], replicated, may hold values from -0.375 to 0.375
- exchange_ints: float32 [16, 16, 160, 160], P('row', None, 'col'), may hold values from -0.0024414062 to 0.0024414062
- fock_occ: float32 [16, 16], replicated, may hold values from -1.5 to 1.5
- fock_vir: float32 [160, 160], replicated, may hold values from -0.5 to 0.5
- eps_occ: float32 [16], replicated, may hold values from -2 to -0.5
- eps_vir: float32 [160], replicated, may hold values from 0.3 to 3
Outputs:
- update: float32 [16, 16, 160, 160], P('row', 'col')
Inputs may be any that keep to these rules, and one draw needn't show every extreme that they name: amplitudes[i, j, a, b] equals amplitudes[j, i, b, a].
All inputs are finite; a program needn't handle non-finite values.
Results may differ from a plain program's by a relative error of at most 0.000064.
Values sent between devices are 32-bit elements; how exact they have to be, the bound alone decides.
A program may use at most 256 MiB of HBM per device.

v0:
```python
import jax
import jax.numpy as jnp
from jax import lax
from jax.sharding import PartitionSpec as P

def on_device(amplitudes, vvvv, hole_ints, exchange_ints, fock_occ, fock_vir, eps_occ, eps_vir):
    high = lax.Precision.HIGH
    rows_n = lax.axis_size("row")
    cols_n = lax.axis_size("col")
    row = lax.axis_index("row")
    col = lax.axis_index("col")
    first_count, second_count, virtual = amplitudes.shape[:3]
    occupied = fock_occ.shape[0]
    pairs_n = occupied * occupied
    a_count = vvvv.shape[0]
    c_count = vvvv.shape[2]
    k_count = exchange_ints.shape[0]

    split = lax.all_to_all(amplitudes, "col", split_axis=2, concat_axis=1, tiled=True)
    split = split.reshape(first_count * occupied, c_count * virtual)
    gathered = lax.all_gather(split, "row", axis=0, tiled=True)
    gathered = gathered.reshape(occupied, occupied, c_count, virtual)

    chi_part = lax.dot_general(
        gathered, exchange_ints, (((2, 3), (2, 3)), ((), ())), precision=high
    )
    chi_part = chi_part.reshape(pairs_n, k_count * occupied).T
    chi_all = lax.all_gather(chi_part, ("row", "col"), axis=0)
    chi = chi_all.reshape(rows_n, cols_n, k_count * occupied, pairs_n).sum(axis=1)
    delta = jnp.eye(occupied, dtype=fock_occ.dtype)
    known = hole_ints - delta[:, None, :, None] * fock_occ[None, :, None, :]
    mixing = chi.reshape(pairs_n, pairs_n) + known.reshape(pairs_n, pairs_n)

    mine = lax.dynamic_slice_in_dim(gathered, row * a_count, a_count, axis=3)
    mine = mine.transpose(1, 0, 3, 2).reshape(pairs_n, a_count, c_count)
    placed = lax.dynamic_update_slice_in_dim(
        jnp.zeros((pairs_n, a_count, virtual), mine.dtype), mine, col * c_count, axis=2
    )

    part = lax.dot_general(gathered, vvvv, (((2, 3), (2, 3)), ((), ())), precision=high)
    hole = lax.dot_general(mixing, placed, (((0,), (0,)), ((), ())), precision=high)
    part = part + hole.reshape(part.shape)
    part = part.transpose(1, 0, 2, 3).reshape(occupied, occupied, a_count * virtual)
    raw = lax.psum_scatter(part, "col", scatter_dimension=0, tiled=True)
    raw = raw.reshape(second_count, rows_n, first_count, a_count * virtual)
    raw = raw.transpose(1, 2, 0, 3)
    raw = lax.all_to_all(raw, "row", split_axis=0, concat_axis=0, tiled=True)
    raw = raw.transpose(1, 2, 0, 3).reshape(first_count, second_count, virtual * virtual)

    ratio = second_count // first_count
    others = []
    for turn in range(ratio):
        route = []
        for r in range(rows_n):
            for q in range(cols_n):
                m = (r + turn) % ratio
                route.append((r * cols_n + q, (q * ratio + m) * cols_n + r // ratio))
        m = lax.rem(row + turn, ratio)
        block = lax.dynamic_slice_in_dim(raw, m * first_count, first_count, axis=1)
        others.append(lax.ppermute(block, ("row", "col"), route))
    stacked = jnp.stack(others)
    order = jnp.stack([lax.rem(row - m + ratio, ratio) for m in range(ratio)])
    other = stacked[order].reshape(ratio, first_count, first_count, virtual, virtual)
    other = other.transpose(2, 0, 1, 4, 3)
    other = other.reshape(first_count, second_count, virtual, virtual)
    total = raw.reshape(first_count, second_count, virtual, virtual) + other
    total = total + jnp.einsum("ijac,cb->ijab", amplitudes, fock_vir, precision=high)
    total = total + jnp.einsum("ac,ijcb->ijab", fock_vir, amplitudes, precision=high)
    energy_rows = lax.dynamic_slice_in_dim(eps_occ, row * first_count, first_count)
    energy_cols = lax.dynamic_slice_in_dim(eps_occ, col * second_count, second_count)
    denominator = (
        energy_rows[:, None, None, None]
        + energy_cols[None, :, None, None]
        - eps_vir[None, None, :, None]
        - eps_vir[None, None, None, :]
    )
    return total / denominator


def solution(mesh):
    in_specs = (
        P("row", "col", None, None),
        P("row", None, "col", None),
        P(),
        P("row", None, "col", None),
        P(),
        P(),
        P(),
        P(),
    )
    out_specs = P("row", "col", None, None)
    return jax.shard_map(
        on_device, mesh=mesh, in_specs=in_specs, out_specs=out_specs, check_vma=False
    )
```

profile of v0, /device:TPU:3, one launch (start us, length us, event | category | flops | bytes accessed | tf_op | source)
XLA Modules:
  0.0 437.8 jit_solution(7601765832758243148)
XLA Ops:
  6.5 0.0 copy-start
  6.5 0.0 all-gather.4.cloned.1.call-start
  6.5 2.2 copy.44
  8.7 18.8 %all_to_all.20 = f32[2,4,160,160]{3,1,0,2:T(4,128)S(1)} all-to-all(f32[2,4,160,160]{3,1,0,2:T(4,128)S(1)} %copy.44), channel_id=1, replica_groups=mesh['row'=8,'col'=4] {'col'}, dimensions={2} | all-to-all | bytes 1638400 | tf_op jit(solution)/shard_map/all_to_all | solution.py:19
  27.5 0.4 copy.80
  27.9 0.0 copy-start.4
  27.9 1.5 reshape.174
  29.4 0.0 all-gather.4.cloned.1.call-update
  29.4 0.0 all-gather.6.cloned.1.call-start
  29.5 0.0 copy-done.4
  29.5 1.8 multiply_subtract_fusion
  31.3 1.6 reshape.178
  32.9 0.0 copy-start.3
  32.9 65.4 %all-gather.4.cloned.1.call-done = f32[256,6400]{1,0:T(8,128)} async-done(((f32[32,6400]{1,0:T(8,128)}), f32[256,6400]{1,0:T(8,128)}) %all-gather.4.cloned.1.call-update) | async-done | bytes 6553616 | tf_op jit(solution)/shard_map/all_gather | solution.py:21
  98.2 8.2 %copy.48 = f32[256,6400]{0,1:T(8,128)} copy(f32[256,6400]{1,0:T(8,128)} %all-gather.4.cloned.1.call-done) | data formatting | bytes 13107200 | tf_op jit(solution)/shard_map/all_gather | solution.py:21
  106.4 0.0 copy-done.3
  106.4 5.6 %fusion.13 = f32[32,256]{1,0:T(8,128)} fusion(f32[256,40,160]{0,2,1:T(8,128)} %bitcast.73, f32[32,40,160]{2,1,0:T(8,128)S(1)} %bitcast.83), kind=kOutput, calls=%fused_computation.18 | convolution fusion | flops 314572800 | bytes 7405568 | tf_op jit(solution)/shard_map/dot_general | solution.py:24
  112.0 0.0 all-gather.6.cloned.1.call-update
  112.0 0.0 reduce-scatter.2.cloned.1.call-start
  112.1 11.0 %reshape.175 = f32[16,16,40,160]{3,2,1,0:T(8,128)} reshape(f32[256,6400]{1,0:T(8,128)} %all-gather.4.cloned.1.call-done) | data formatting | bytes 13107200 | tf_op jit(solution)/shard_map/reshape | solution.py:22
  123.1 129.2 %fusion = f32[16,16,20,160,1]{3,1,4,2,0:T(8,128)} fusion(f32[20,160,40,160]{3,2,1,0:T(8,128)} %param.9, f32[16,16,40,160,1]{3,2,1,0,4:T(8,128)} %bitcast.74), kind=kOutput, calls=%fused_computation.1 | convolution fusion | flops 31457280000 | bytes 91750400 | tf_op jit(solution)/shard_map/dot_general | solution.py:40
  252.3 7.7 %dynamic-slice_bitcast_fusion = f32[16,16,20,40]{2,3,0,1:T(8,128)} fusion(f32[16,16,40,160]{3,2,1,0:T(8,128)} %reshape.175, s32[]{:T(128)S(6)} %select_n.28), kind=kLoop, calls=%fused_computation.7 | loop fusion | bytes 1638404 | tf_op jit(solution)/shard_map/transpose | solution.py:35
  259.9 4.6 %copy.51 = f32[16,16,20,40]{3,1,0,2:T(8,128)S(1)} copy(f32[16,16,20,40]{2,3,0,1:T(8,128)} %dynamic-slice_bitcast_fusion) | data formatting | bytes 1638400 | tf_op jit(solution)/shard_map/transpose | solution.py:35
  264.5 1.7 copy.52
  266.3 0.0 copy-start.2
  266.3 0.3 broadcast_in_dim.2
  266.6 0.8 copy-done.2
  267.4 0.1 constant_dynamic-update-slice_fusion
  267.5 0.0 all-gather.6.cloned.1.call-done
  267.5 2.0 reduce_sum.9
  269.5 1.8 bitcast_add_fusion.1
  271.3 1.8 copy.50
  273.1 5.2 %fusion.4 = f32[16,16,20,160]{3,0,2,1:T(8,128)S(1)} fusion(f32[16,16,20,160,1]{3,1,4,2,0:T(8,128)} %fusion, f32[16,16,256,1]{2,1,3,0:T(8,128)} %bitcast.84, f32[256,20,160]{0,2,1:T(8,128)S(1)} %constant_dynamic-update-slice_fusion), kind=kOutput, calls=%fused_computation.6 | convolution fusion | flops 1259110400 | bytes 10092544 | tf_op jit(solution)/shard_map/dot_general | solution.py:41
  278.3 5.7 %copy.53 = f32[16,16,20,160]{3,2,1,0:T(8,128)} copy(f32[16,16,20,160]{3,0,2,1:T(8,128)S(1)} %fusion.4) | data formatting | bytes 6553600 | tf_op jit(solution)/shard_map/add | solution.py:42
  284.1 6.1 %reshape.180 = f32[16,16,3200]{2,1,0:T(8,128)} reshape(f32[16,16,20,160]{3,2,1,0:T(8,128)} %copy.53) | data formatting | bytes 6553600 | tf_op jit(solution)/shard_map/reshape | solution.py:43
  290.2 0.0 reduce-scatter.2.cloned.1.call-update
  290.2 0.0 copy-start.6
  290.2 43.2 %reduce-scatter.2.cloned.1.call-done = f32[4,16,3200]{2,1,0:T(8,128)} async-done(((f32[16,16,3200]{2,1,0:T(8,128)}), f32[4,16,3200]{2,1,0:T(8,128)}) %reduce-scatter.2.cloned.1.call-update) | async-done | bytes 819216 | tf_op jit(solution)/shard_map/reduce_scatter | solution.py:44
  333.4 2.4 copy.54
  335.8 5.6 %all-to-all-start.1 = ((f32[8,2,4,3200]{3,2,1,0:T(4,128)}), f32[8,2,4,3200]{3,2,1,0:T(4,128)S(1)}, u32[]{:S(2)}, u32[]{:S(2)}) async-start(f32[8,2,4,3200]{3,2,1,0:T(4,128)} %bitcast.20), calls=%async_computation.2 | async-start | bytes 1638400 | tf_op jit(solution)/shard_map/all_to_all | solution.py:47
  341.4 0.0 copy-done.6
  341.4 0.1 dynamic_slice.19
  341.5 0.1 dynamic_slice.18
  341.5 0.1 fusion.19
  341.6 20.4 %all-to-all-done.1 = f32[8,2,4,3200]{3,2,1,0:T(4,128)S(1)} async-done(((f32[8,2,4,3200]{3,2,1,0:T(4,128)}), f32[8,2,4,3200]{3,2,1,0:T(4,128)S(1)}, u32[]{:S(2)}, u32[]{:S(2)}) %all-to-all-start.1) | async-done | bytes 819232 | tf_op jit(solution)/shard_map/all_to_all | solution.py:47
  362.1 0.1 copy.68
  362.1 0.4 constant_dynamic-slice_fusion.1
  362.5 2.2 collective-permute-start
  364.7 3.6 collective-permute-start.1
  368.2 0.1 broadcast_add_fusion
  368.3 0.0 copy-done.5
  368.3 0.1 broadcast_subtract_fusion
  368.4 0.2 copy.55
  368.5 1.6 reshape_reshape.3
  370.2 40.7 %collective-permute-done = f32[2,2,25600]{2,1,0:T(2,128)S(1)} collective-permute-done((f32[2,2,25600]{2,1,0:T(2,128)S(1)}, f32[2,2,25600]{2,1,0:T(2,128)S(1)}, u32[]{:S(2)}, u32[]{:S(2)}) %collective-permute-start) | collective-permute-done | bytes 409632 | tf_op jit(solution)/shard_map/ppermute | solution.py:60
  410.9 9.5 %collective-permute-done.1 = f32[2,2,25600]{2,1,0:T(2,128)S(1)} collective-permute-done((f32[2,2,25600]{2,1,0:T(2,128)S(1)}, f32[2,2,25600]{2,1,0:T(2,128)S(1)}, u32[]{:S(2)}, u32[]{:S(2)}) %collective-permute-start.1) | collective-permute-done | bytes 409632 | tf_op jit(solution)/shard_map/ppermute | solution.py:60
  420.4 0.4 pad_maximum_fusion
  420.7 2.3 gather_fusion
  423.0 2.2 reshape.183
  425.2 1.7 copy.57
  426.9 0.0 copy-done
  426.9 0.0 copy-done.1
  426.9 2.4 convolution_add_fusion
  429.3 1.9 fusion.10
  (4 shorter events, 0.0 us)
Async XLA Ops:
  6.5 420.3 %copy-start = (f32[160,160]{1,0:T(8,128)S(1)}, f32[160,160]{1,0:T(8,128)}, u32[]{:S(2)}) copy-start(f32[160,160]{1,0:T(8,128)} %param.13) | copy-start | bytes 307204
  6.5 91.7 %all-gather.4.cloned.1.call-start = ((), (), s32[]{:S(2)}) async-start(), calls=%async_computation.3 | async-start | bytes 7372800 | tf_op jit(solution)/shard_map/all_gather | solution.py:21
  27.9 1.6 copy-start.4
  29.4 238.1 %all-gather.6.cloned.1.call-start = ((), (), s32[]{:S(2)}) async-start(), calls=%async_computation.5 | async-start | bytes 1081344 | tf_op jit(solution)/shard_map/all_gather | solution.py:28
  32.9 73.5 %copy-start.3 = (f32[2,16,40,160]{3,2,1,0:T(8,128)S(1)}, f32[2,16,40,160]{3,2,1,0:T(8,128)}, u32[]{:S(2)}) copy-start(f32[2,16,40,160]{3,2,1,0:T(8,128)} %param.11) | copy-start | bytes 2457604
  112.0 221.4 %reduce-scatter.2.cloned.1.call-start = ((), (), s32[]{:S(2)}) async-start(), calls=%async_computation.4 | async-start | bytes 4096000 | tf_op jit(solution)/shard_map/reduce_scatter | solution.py:44
  266.3 1.1 copy-start.2
  290.2 51.2 %copy-start.6 = (f32[16]{0:T(128)S(1)}, f32[16]{0:T(128)}, u32[]{:S(2)}) copy-start(f32[16]{0:T(128)} %param.14) | copy-start | bytes 196
  335.8 32.5 %copy-start.5 = (f32[160]{0:T(256)S(1)}, f32[160]{0:T(256)}, u32[]{:S(2)}) copy-start(f32[160]{0:T(256)} %param.15) | copy-start | bytes 1924
  335.8 26.3 %all-to-all-start.1 = ((f32[8,2,4,3200]{3,2,1,0:T(4,128)}), f32[8,2,4,3200]{3,2,1,0:T(4,128)S(1)}, u32[]{:S(2)}, u32[]{:S(2)}) async-start(f32[8,2,4,3200]{3,2,1,0:T(4,128)} %bitcast.20), calls=%async_computation.2 | async-start | bytes 1638400 | tf_op jit(solution)/shard_map/all_to_all | solution.py:47
  362.5 48.4 %collective-permute-start = (f32[2,2,25600]{2,1,0:T(2,128)S(1)}, f32[2,2,25600]{2,1,0:T(2,128)S(1)}, u32[]{:S(2)}, u32[]{:S(2)}) collective-permute-start(f32[2,2,25600]{2,1,0:T(2,128)S(1)} %get-tuple-element.5), channel_id=1, source_target_pairs={{0,0},{1,8},{2,16},{3,24},{4,4},{5,12},{6,20},{7,28},{8,1},{9,9},{... | collective-permute-start | bytes 1228808 | tf_op jit(solution)/shard_map/ppermute | solution.py:60
  364.7 55.7 %collective-permute-start.1 = (f32[2,2,25600]{2,1,0:T(2,128)S(1)}, f32[2,2,25600]{2,1,0:T(2,128)S(1)}, u32[]{:S(2)}, u32[]{:S(2)}) collective-permute-start(f32[2,2,25600]{2,1,0:T(2,128)S(1)} %get-tuple-element.6), channel_id=1, source_target_pairs={{0,4},{1,12},{2,20},{3,28},{4,0},{5,8},{6,16},{7,24},{8,5},{9,13},... | collective-permute-start | bytes 1228808 | tf_op jit(solution)/shard_map/ppermute | solution.py:60
  423.0 3.9 copy-start.1
Sparse Core Ops, SparseCore 0:
  29.5 68.6 all-gather.3
  112.2 52.1 all-gather.5
  290.4 43.0 reduce-scatter.1
where the time goes:
time: 439 us; the launch traced here: 438 us
  waiting for transfers between devices  179 us (41%)
  matrix products  144 us (33%)
  local copies, waits for them, and re-layouts  64.5 us (15%)
  blocking collectives  18.8 us (4%)
  between operations  13.3 us (3%)
  starting transfers between devices  11.4 us (3%)
  other arithmetic  6.22 us (1%)
    dot_general x1, matrix products, on_device(): lax.dot_general(gathered, vvvv, (((2, 3), (2, 3)), ((), ())), precision=h...  129 us
    all_gather x1, waiting for transfers between devices, on_device(): gathered = lax.all_gather(split, 'row', axis=0, tiled=True)  65.4 us
    ppermute x2, waiting for transfers between devices, on_device(): others.append(lax.ppermute(block, ('row', 'col'), route))  50.2 us
    reduce_scatter x1, waiting for transfers between devices, on_device(): raw = lax.psum_scatter(part, 'col', scatter_dimension=0, tiled=True)  43.2 us
    all_to_all x1, waiting for transfers between devices, on_device(): raw = lax.all_to_all(raw, 'row', split_axis=0, concat_axis=0, tiled=True)  20.4 us
    all_to_all x1, blocking collectives, on_device(): lax.all_to_all(amplitudes, 'col', split_axis=2, concat_axis=1, tiled=True)  18.8 us
    transpose x2, local copies, waits for them, and re-layouts, on_device(): mine = mine.transpose(1, 0, 3, 2).reshape(pairs_n, a_count, c_count)  12.3 us
    reshape x1, local copies, waits for them, and re-layouts, on_device(): gathered = gathered.reshape(occupied, occupied, c_count, virtual)  11 us
  transfers between devices with their start and end apart: 6, of which 5 were waited for; matrix products, arithmetic and copies ran while one was open for 37% of the time, Pallas kernels for 0%

commit v1 on v0

--- a/solution.py
+++ b/solution.py
@@ -32,16 +32,20 @@
     mixing = chi.reshape(pairs_n, pairs_n) + known.reshape(pairs_n, pairs_n)
 
     mine = lax.dynamic_slice_in_dim(gathered, row * a_count, a_count, axis=3)
-    mine = mine.transpose(1, 0, 3, 2).reshape(pairs_n, a_count, c_count)
-    placed = lax.dynamic_update_slice_in_dim(
-        jnp.zeros((pairs_n, a_count, virtual), mine.dtype), mine, col * c_count, axis=2
-    )
+    mine = mine.transpose(1, 0, 3, 2).reshape(pairs_n, a_count * c_count)
+    placed = lax.all_gather(mine, "col", axis=0)
+    placed = placed.reshape(cols_n, pairs_n, a_count, c_count).transpose(1, 2, 0, 3)
+    placed = placed.reshape(pairs_n, a_count * virtual)
 
     part = lax.dot_general(gathered, vvvv, (((2, 3), (2, 3)), ((), ())), precision=high)
-    hole = lax.dot_general(mixing, placed, (((0,), (0,)), ((), ())), precision=high)
-    part = part + hole.reshape(part.shape)
     part = part.transpose(1, 0, 2, 3).reshape(occupied, occupied, a_count * virtual)
     raw = lax.psum_scatter(part, "col", scatter_dimension=0, tiled=True)
+    chosen = lax.dynamic_slice_in_dim(
+        mixing.reshape(pairs_n, occupied, occupied), col * second_count, second_count, axis=2
+    )
+    chosen = chosen.transpose(0, 2, 1).reshape(pairs_n, second_count * occupied)
+    hole = lax.dot_general(chosen, placed, (((0,), (0,)), ((), ())), precision=high)
+    raw = raw + hole.reshape(raw.shape)
     raw = raw.reshape(second_count, rows_n, first_count, a_count * virtual)
     raw = raw.transpose(1, 2, 0, 3)
     raw = lax.all_to_all(raw, "row", split_axis=0, concat_axis=0, tiled=True)

time: 439 us -> 434 us (0.989)
  local copies, waits for them, and re-layouts: 64.5 us -> 70.2 us
    transpose x2 -> x4, local copies, waits for them, and re-layouts: 12.3 us -> 23 us  [the longest x2 12.4 us: on_device(): mine = mine.transpose(1, 0, 3, 2).reshape(pairs_n, a_count * c_count)]
    reduce_scatter x1, waiting for transfers between devices: 43.2 us -> 35.2 us  [on_device(): raw = lax.psum_scatter(part, 'col', scatter_dimension=0, tiled=True)]
    add x1 -> x0, local copies, waits for them, and re-layouts: 5.74 us -> none  [on_device(): part = part + hole.reshape(part.shape)]
  transfers between devices with their start and end apart: 6 -> 7, of which waited for: 5 -> 5; matrix products, arithmetic and copies ran while one was open for 37% -> 42% of each run, Pallas kernels for 0% -> 0%
where the time goes in v1:
time: 434 us; the launch traced here: 433 us
  waiting for transfers between devices  175 us (40%)
  matrix products  142 us (33%)
  local copies, waits for them, and re-layouts  70.2 us (16%)
  blocking collectives  18.8 us (4%)
  between operations  13.3 us (3%)
  starting transfers between devices  11.6 us (3%)
    dot_general x1, matrix products, on_device(): lax.dot_general(gathered, vvvv, (((2, 3), (2, 3)), ((), ())), precision=h...  129 us
    all_gather x1, waiting for transfers between devices, on_device(): gathered = lax.all_gather(split, 'row', axis=0, tiled=True)  68.8 us
    ppermute x2, waiting for transfers between devices, on_device(): others.append(lax.ppermute(block, ('row', 'col'), route))  50.2 us
    reduce_scatter x1, waiting for transfers between devices, on_device(): raw = lax.psum_scatter(part, 'col', scatter_dimension=0, tiled=True)  35.2 us
    all_to_all x1, waiting for transfers between devices, on_device(): raw = lax.all_to_all(raw, 'row', split_axis=0, concat_axis=0, tiled=True)  20.4 us
    all_to_all x1, blocking collectives, on_device(): lax.all_to_all(amplitudes, 'col', split_axis=2, concat_axis=1, tiled=True)  18.8 us
    transpose x2, local copies, waits for them, and re-layouts, on_device(): mine = mine.transpose(1, 0, 3, 2).reshape(pairs_n, a_count * c_count)  12.4 us
    reshape x1, local copies, waits for them, and re-layouts, on_device(): gathered = gathered.reshape(occupied, occupied, c_count, virtual)  11 us
  transfers between devices with their start and end apart: 7, of which 5 were waited for; matrix products, arithmetic and copies ran while one was open for 42% of the time, Pallas kernels for 0%

profile of v1, /device:TPU:3, one launch (start us, length us, event | category | flops | bytes accessed | tf_op | source)
XLA Modules:
  0.0 432.6 jit_solution(12215672303684575956)
XLA Ops:
  6.5 0.0 copy-start
  6.5 0.0 all-gather.5.cloned.1.call-start
  6.5 2.2 copy.47
  8.7 18.8 %all_to_all.20 = f32[2,4,160,160]{3,1,0,2:T(4,128)S(1)} all-to-all(f32[2,4,160,160]{3,1,0,2:T(4,128)S(1)} %copy.47), channel_id=1, replica_groups=mesh['row'=8,'col'=4] {'col'}, dimensions={2} | all-to-all | bytes 1638400 | tf_op jit(solution)/shard_map/all_to_all | solution.py:19
  27.5 0.4 copy.99
  27.9 1.5 reshape.183
  29.4 0.0 all-gather.5.cloned.1.call-update
  29.4 0.0 copy-start.3
  29.4 0.0 all-gather.9.cloned.1.call-start
  29.5 68.8 %all-gather.5.cloned.1.call-done = f32[256,6400]{1,0:T(8,128)} async-done(((f32[32,6400]{1,0:T(8,128)}), f32[256,6400]{1,0:T(8,128)}) %all-gather.5.cloned.1.call-update) | async-done | bytes 6553616 | tf_op jit(solution)/shard_map/all_gather | solution.py:21
  98.2 8.2 %copy.52 = f32[256,6400]{0,1:T(8,128)} copy(f32[256,6400]{1,0:T(8,128)} %all-gather.5.cloned.1.call-done) | data formatting | bytes 13107200 | tf_op jit(solution)/shard_map/all_gather | solution.py:21
  106.4 0.0 copy-done.3
  106.4 5.6 %fusion.13 = f32[32,256]{1,0:T(8,128)} fusion(f32[256,40,160]{0,2,1:T(8,128)} %bitcast.75, f32[32,40,160]{2,1,0:T(8,128)S(1)} %bitcast.87), kind=kOutput, calls=%fused_computation.16 | convolution fusion | flops 314572800 | bytes 7405568 | tf_op jit(solution)/shard_map/dot_general | solution.py:24
  112.0 0.0 all-gather.9.cloned.1.call-update
  112.0 0.0 all-gather.7.cloned.1.call-start
  112.1 11.0 %reshape.184 = f32[16,16,40,160]{3,2,1,0:T(8,128)} reshape(f32[256,6400]{1,0:T(8,128)} %all-gather.5.cloned.1.call-done) | data formatting | bytes 13107200 | tf_op jit(solution)/shard_map/reshape | solution.py:22
  123.1 7.8 %dynamic-slice_bitcast_fusion = f32[16,16,20,40]{2,3,0,1:T(8,128)} fusion(f32[16,16,40,160]{3,2,1,0:T(8,128)} %reshape.184, s32[]{:T(128)S(6)} %select_n.27), kind=kLoop, calls=%fused_computation.5 | loop fusion | bytes 1638404 | tf_op jit(solution)/shard_map/transpose | solution.py:35
  130.8 4.7 %copy.57 = f32[16,16,20,40]{3,2,1,0:T(8,128)S(1)} copy(f32[16,16,20,40]{2,3,0,1:T(8,128)} %dynamic-slice_bitcast_fusion) | data formatting | bytes 1638400 | tf_op jit(solution)/shard_map/transpose | solution.py:35
  135.5 1.7 all_gather_reshape.3
  137.2 2.4 copy.58
  139.6 0.0 all-gather.7.cloned.1.call-update
  139.6 0.2 reduce-scatter.2.cloned.1.call-start
  139.8 129.2 %fusion.4 = f32[16,16,20,160]{3,0,2,1:T(8,128)} fusion(f32[20,160,40,160]{3,2,1,0:T(8,128)} %param.9, f32[16,16,40,160,1]{3,2,1,0,4:T(8,128)} %bitcast.76), kind=kOutput, calls=%fused_computation.7 | convolution fusion | flops 31457280000 | bytes 91750400 | tf_op jit(solution)/shard_map/dot_general | solution.py:40
  269.0 8.2 %copy.51 = f32[16,16,20,160]{3,2,1,0:T(8,128)} copy(f32[16,16,20,160]{3,0,2,1:T(8,128)} %fusion.4) | data formatting | bytes 6553600 | tf_op jit(solution)/shard_map/transpose | solution.py:41
  277.3 6.2 %reshape.185 = f32[16,16,3200]{2,1,0:T(8,128)} reshape(f32[16,16,20,160]{3,2,1,0:T(8,128)} %copy.51) | data formatting | bytes 6553600 | tf_op jit(solution)/shard_map/reshape | solution.py:41
  283.5 0.0 reduce-scatter.2.cloned.1.call-update
  283.5 1.5 copy-done.2
  285.0 0.0 copy-done.4
  285.1 0.2 multiply_subtract_fusion
  285.3 0.6 constant_dynamic-slice_fusion.2
  285.9 1.0 copy.78
  287.0 1.3 reduce_sum.9
  288.3 0.4 copy.54
  288.7 0.3 reshape.187
  289.1 0.0 all-gather.7.cloned.1.call-done
  289.1 2.4 copy.59
  291.5 35.2 %reduce-scatter.2.cloned.1.call-done = f32[4,16,3200]{2,1,0:T(8,128)} async-done(((f32[16,16,3200]{2,1,0:T(8,128)}), f32[4,16,3200]{2,1,0:T(8,128)}) %reduce-scatter.2.cloned.1.call-update) | async-done | bytes 819216 | tf_op jit(solution)/shard_map/reduce_scatter | solution.py:42
  326.7 2.7 convolution_add_fusion
  329.4 0.0 copy-start.6
  329.5 1.2 copy.77
  330.7 5.6 %all-to-all-start.1 = ((f32[8,2,4,3200]{3,2,1,0:T(4,128)}), f32[8,2,4,3200]{3,2,1,0:T(4,128)S(1)}, u32[]{:S(2)}, u32[]{:S(2)}) async-start(f32[8,2,4,3200]{3,2,1,0:T(4,128)} %bitcast.22), calls=%async_computation.2 | async-start | bytes 1638400 | tf_op jit(solution)/shard_map/all_to_all | solution.py:51
  336.3 0.0 copy-done.6
  336.3 0.1 dynamic_slice.23
  336.3 0.1 dynamic_slice.22
  336.4 0.1 fusion.22
  336.5 20.4 %all-to-all-done.1 = f32[8,2,4,3200]{3,2,1,0:T(4,128)S(1)} async-done(((f32[8,2,4,3200]{3,2,1,0:T(4,128)}), f32[8,2,4,3200]{3,2,1,0:T(4,128)S(1)}, u32[]{:S(2)}, u32[]{:S(2)}) %all-to-all-start.1) | async-done | bytes 819232 | tf_op jit(solution)/shard_map/all_to_all | solution.py:51
  356.9 0.1 copy.79
  357.0 0.4 constant_dynamic-slice_fusion.1
  357.4 2.2 collective-permute-start
  359.6 3.6 collective-permute-start.1
  363.1 0.1 broadcast_add_fusion
  363.2 0.0 copy-done.5
  363.2 0.1 broadcast_subtract_fusion
  363.3 0.2 copy.62
  363.4 1.6 reshape_reshape.3
  365.1 40.7 %collective-permute-done = f32[2,2,25600]{2,1,0:T(2,128)S(1)} collective-permute-done((f32[2,2,25600]{2,1,0:T(2,128)S(1)}, f32[2,2,25600]{2,1,0:T(2,128)S(1)}, u32[]{:S(2)}, u32[]{:S(2)}) %collective-permute-start) | collective-permute-done | bytes 409632 | tf_op jit(solution)/shard_map/ppermute | solution.py:64
  405.8 9.5 %collective-permute-done.1 = f32[2,2,25600]{2,1,0:T(2,128)S(1)} collective-permute-done((f32[2,2,25600]{2,1,0:T(2,128)S(1)}, f32[2,2,25600]{2,1,0:T(2,128)S(1)}, u32[]{:S(2)}, u32[]{:S(2)}) %collective-permute-start.1) | collective-permute-done | bytes 409632 | tf_op jit(solution)/shard_map/ppermute | solution.py:64
  415.2 0.4 pad_maximum_fusion
  415.6 2.3 gather_fusion
  417.9 2.2 reshape.194
  420.1 1.7 copy.64
  421.8 0.0 copy-done.1
  421.8 2.4 convolution_add_fusion.1
  424.2 1.9 fusion.10
  (9 shorter events, 0.1 us)
Async XLA Ops:
  6.5 415.2 %copy-start = (f32[160,160]{1,0:T(8,128)S(1)}, f32[160,160]{1,0:T(8,128)}, u32[]{:S(2)}) copy-start(f32[160,160]{1,0:T(8,128)} %param.13) | copy-start | bytes 307204
  6.5 91.7 %all-gather.5.cloned.1.call-start = ((), (), s32[]{:S(2)}) async-start(), calls=%async_computation.3 | async-start | bytes 7372800 | tf_op jit(solution)/shard_map/all_gather | solution.py:21
  29.4 77.0 %copy-start.3 = (f32[2,16,40,160]{3,2,1,0:T(8,128)S(1)}, f32[2,16,40,160]{3,2,1,0:T(8,128)}, u32[]{:S(2)}) copy-start(f32[2,16,40,160]{3,2,1,0:T(8,128)} %param.11) | copy-start | bytes 2457604
  29.4 257.5 %all-gather.9.cloned.1.call-start = ((), (), s32[]{:S(2)}) async-start(), calls=%async_computation.6 | async-start | bytes 1081344 | tf_op jit(solution)/shard_map/all_gather | solution.py:28
  112.0 177.0 %all-gather.7.cloned.1.call-start = ((), (), s32[]{:S(2)}) async-start(), calls=%async_computation.5 | async-start | bytes 4096000 | tf_op jit(solution)/shard_map/all_gather | solution.py:36
  139.6 187.1 %reduce-scatter.2.cloned.1.call-start = ((), (), s32[]{:S(2)}) async-start(), calls=%async_computation.4 | async-start | bytes 4096000 | tf_op jit(solution)/shard_map/reduce_scatter | solution.py:42
  283.5 1.6 copy-start.2
  283.5 1.6 copy-start.4
  329.4 6.8 %copy-start.6 = (f32[16]{0:T(128)S(1)}, f32[16]{0:T(128)}, u32[]{:S(2)}) copy-start(f32[16]{0:T(128)} %param.14) | copy-start | bytes 196
  330.7 32.5 %copy-start.5 = (f32[160]{0:T(256)S(1)}, f32[160]{0:T(256)}, u32[]{:S(2)}) copy-start(f32[160]{0:T(256)} %param.15) | copy-start | bytes 1924
  330.7 26.3 %all-to-all-start.1 = ((f32[8,2,4,3200]{3,2,1,0:T(4,128)}), f32[8,2,4,3200]{3,2,1,0:T(4,128)S(1)}, u32[]{:S(2)}, u32[]{:S(2)}) async-start(f32[8,2,4,3200]{3,2,1,0:T(4,128)} %bitcast.22), calls=%async_computation.2 | async-start | bytes 1638400 | tf_op jit(solution)/shard_map/all_to_all | solution.py:51
  357.4 48.4 %collective-permute-start = (f32[2,2,25600]{2,1,0:T(2,128)S(1)}, f32[2,2,25600]{2,1,0:T(2,128)S(1)}, u32[]{:S(2)}, u32[]{:S(2)}) collective-permute-start(f32[2,2,25600]{2,1,0:T(2,128)S(1)} %get-tuple-element.5), channel_id=1, source_target_pairs={{0,0},{1,8},{2,16},{3,24},{4,4},{5,12},{6,20},{7,28},{8,1},{9,9},{... | collective-permute-start | bytes 1228808 | tf_op jit(solution)/shard_map/ppermute | solution.py:64
  359.6 55.7 %collective-permute-start.1 = (f32[2,2,25600]{2,1,0:T(2,128)S(1)}, f32[2,2,25600]{2,1,0:T(2,128)S(1)}, u32[]{:S(2)}, u32[]{:S(2)}) collective-permute-start(f32[2,2,25600]{2,1,0:T(2,128)S(1)} %get-tuple-element.6), channel_id=1, source_target_pairs={{0,4},{1,12},{2,20},{3,28},{4,0},{5,8},{6,16},{7,24},{8,5},{9,13},... | collective-permute-start | bytes 1228808 | tf_op jit(solution)/shard_map/ppermute | solution.py:64
  417.9 3.9 copy-start.1
Sparse Core Ops, SparseCore 0:
  29.5 68.6 all-gather.4
  112.2 52.1 all-gather.8
  166.2 43.4 all-gather.6
  283.6 43.0 reduce-scatter.1
